TPU v7x, 256 devices: a whole 4x4x8 slice. The times are simulated.
256 devices in a mesh: session: 8 (over x_lo, y), ctx: 32 (over x_hi, z, core).
Axes of the slice: x: 4 (x_hi: 2, x_lo: 2; x = x_hi * 2 + x_lo), y: 4, z: 8, core: 2. Of those that a mesh axis runs over, the one named last changes fastest.
Arguments:
- frames: float32 [49152, 1024], P(('session', 'ctx')), parts along dimension 0, may hold values from -6 to 6
- attend_gain: float32 [1024], replicated, may hold values from 0.25 to 1.75
- query_weight: bfloat16 [1024, 1024], replicated, may hold values from -8 to 8
- key_weight: bfloat16 [1024, 1024], replicated, may hold values from -8 to 8
- value_weight: bfloat16 [1024, 1024], replicated, may hold values from -0.1875 to 0.1875
- output_weight: bfloat16 [1024, 1024], replicated, may hold values from -0.1875 to 0.1875
- mixer_gain: float32 [1024], replicated, may hold values from 0.25 to 1.75
- depthwise: float32 [31, 1024], replicated, may hold values from -1 to 1
- mixer_bias: float32 [1024], replicated, may hold values from -3 to 3
Outputs:
- block_out: float32 [49152, 1024], P(('session', 'ctx')), parts along dimension 0
There are 8 independent parts, one for each index of `session`. A program takes and returns all parts, laid end to end along the dimension named above; an argument that names none is the same for every part. Nothing has to cross between parts.
All inputs are finite; a program needn't handle non-finite values.
Results may differ from a plain program's by a relative error of at most 0.0031.
Values may be sent and summed in bfloat16 or wider, within the bound.
A program may use at most 256 MiB of HBM per device.

v0:
```python
import jax
import jax.numpy as jnp
from jax import lax
from jax.sharding import PartitionSpec as P

HEADS = 16
KERNEL = 31


def with_halo(block, sides, width):
    for axis, dim in sides:
        count = lax.axis_size(axis)
        forward = [(i, i + 1) for i in range(count - 1)]
        backward = [(target, source) for source, target in forward]
        low = lax.ppermute(
            lax.slice_in_dim(block, block.shape[dim] - width, None, axis=dim), axis, forward
        )
        high = lax.ppermute(lax.slice_in_dim(block, 0, width, axis=dim), axis, backward)
        block = jnp.concatenate([low, block, high], axis=dim)
    return block


def norm_rows(values_in, gain):
    center = jnp.mean(values_in, axis=1, keepdims=True)
    spread = jnp.mean(jnp.square(values_in - center), axis=1, keepdims=True)
    return (values_in - center) * lax.rsqrt(spread + 1e-05) * gain


def project(source, weight):
    return jnp.dot(source, weight, preferred_element_type=jnp.float32).astype(jnp.bfloat16)


def per_device(
    frames,
    attend_gain,
    query_weight,
    key_weight,
    value_weight,
    output_weight,
    mixer_gain,
    depthwise,
    mixer_bias,
):
    row_count, feature_count = frames.shape
    head_size = feature_count // HEADS
    score_scale = head_size ** (-0.5)
    normed = norm_rows(frames, attend_gain).astype(jnp.bfloat16)
    query_heads = project(normed, query_weight).reshape(row_count, HEADS, head_size)
    key_rows = project(normed, key_weight)
    value_rows = project(normed, value_weight)
    key_block = lax.all_gather(key_rows, "ctx", axis=0, tiled=True)
    highest = jnp.full((HEADS, row_count), -1e30, jnp.float32)
    block_rows = key_block.shape[0]
    key_heads = key_block.reshape(block_rows, HEADS, head_size)
    value_heads = lax.all_gather(value_rows, "ctx", axis=0, tiled=True).reshape(
        block_rows, HEADS, head_size
    )
    scores = (
        jnp.einsum("qhd,khd->hqk", query_heads, key_heads, preferred_element_type=jnp.float32)
        * score_scale
    )
    new_high = jnp.maximum(highest, jnp.max(scores, axis=2))
    weights = jnp.exp(scores - new_high[:, :, None])
    partial_sum = jnp.einsum(
        "hqk,khd->qhd",
        weights.astype(jnp.bfloat16),
        value_heads,
        preferred_element_type=jnp.float32,
    )
    totals = jnp.sum(weights, axis=2)
    running = partial_sum
    highest, totals, running = (new_high, totals, running)
    context = (
        (running / jnp.transpose(totals)[:, :, None])
        .reshape(row_count, feature_count)
        .astype(jnp.bfloat16)
    )
    attended = frames + jnp.dot(context, output_weight, preferred_element_type=jnp.float32)
    mixer_in = norm_rows(attended, mixer_gain)
    half_width = KERNEL // 2
    padded = with_halo(mixer_in, (("ctx", 0),), half_width)
    convolved = jnp.zeros_like(mixer_in) + mixer_bias
    for tap_index in range(KERNEL):
        convolved = convolved + padded[tap_index : tap_index + row_count] * depthwise[tap_index]
    return attended + jax.nn.silu(convolved)


def solution(mesh):
    in_specs = (P(("session", "ctx"), None), P(), P(), P(), P(), P(), P(), P(), P())
    out_specs = P(("session", "ctx"), None)
    return jax.shard_map(
        per_device, mesh=mesh, in_specs=in_specs, out_specs=out_specs, check_vma=False
    )
```

profile of v0, /device:TPU:1, one launch (start us, length us, event | category | flops | bytes accessed | tf_op | source)
XLA Modules:
  0.0 318.0 jit_solution(9778761787293347411)
XLA Ops:
  6.5 1.4 reduce_sum.45
  8.0 1.4 multiply_reduce_fusion.2
  9.3 3.3 %convolution_convert_fusion = bf16[192,1024]{1,0:T(8,128)(2,1)} fusion(bf16[1024,1024]{1,0:T(8,128)(2,1)} %param.12, f32[192,1024]{1,0:T(8,128)} %param.9, f32[1024]{0:T(1024)} %param.10, f32[192]{0:T(256)S(1)} %add_rsqrt_fusion.1, f32[192]{0:T(256)S(1)} %broadcast_multiply_fusion.1), kind=kOutput, calls=%fused_computation.37 | convolution fusion | flops 403636224 | bytes 3282432 | tf_op jit(solution)/shard_map/dot_general | solution.py:30
  12.6 0.0 all-gather.5.cloned.1.call-update
  12.6 0.0 all-gather.3.cloned.1.call-start
  12.7 3.2 %convolution_convert_fusion.2 = bf16[192,1024]{1,0:T(8,128)(2,1)} fusion(bf16[1024,1024]{1,0:T(8,128)(2,1)} %param.13, f32[192,1024]{1,0:T(8,128)} %param.9, f32[1024]{0:T(1024)} %param.10, f32[192]{0:T(256)S(1)} %add_rsqrt_fusion.1, f32[192]{0:T(256)S(1)} %broadcast_multiply_fusion.1), kind=kOutput, calls=%fused_computation.39 | convolution fusion | flops 403636224 | bytes 3282432 | tf_op jit(solution)/shard_map/dot_general | solution.py:30
  15.9 2.5 convolution_convert_fusion.1
  18.4 0.2 copy.14
  18.7 0.1 fusion.106
  18.7 115.4 %all-gather.5.cloned.1.call-done = bf16[6144,1024]{1,0:T(8,128)(2,1)} async-done(((bf16[192,1024]{1,0:T(8,128)(2,1)}), bf16[6144,1024]{1,0:T(8,128)(2,1)}) %all-gather.5.cloned.1.call-update) | async-done | bytes 12582928 | tf_op jit(solution)/shard_map/all_gather | solution.py:51
  134.1 16.7 %copy.15 = bf16[6144,1024]{0,1:T(8,128)(2,1)} copy(bf16[6144,1024]{1,0:T(8,128)(2,1)} %all-gather.5.cloned.1.call-done) | data formatting | bytes 25165824 | tf_op jit(solution)/shard_map/all_gather | solution.py:51
  150.8 30.4 %multiply_reduce_fusion = (f32[16,192]{1,0:T(8,128)S(1)}, f32[16,192,6144]{2,1,0:T(8,128)}) fusion(bf16[192,16,64]{0,2,1:T(8,128)(2,1)S(1)} %bitcast.53, bf16[6144,16,64]{0,2,1:T(8,128)(2,1)} %bitcast.50), kind=kOutput, calls=%fused_computation.1 | convolution fusion | flops 2453664768 | bytes 88485888 | tf_op jit(solution)/shard_map/qhd,khd->hqk/dot_general | solution.py:59
  181.2 25.1 %fusion = f32[16,192]{1,0:T(8,128)S(1)} fusion(f32[16,192,6144]{2,1,0:T(8,128)} %get-tuple-element.39, f32[16,192]{1,0:T(8,128)S(1)} %broadcast_maximum_fusion), kind=kLoop, calls=%fused_computation.2 | loop fusion | flops 56620032 | bytes 75522048 | tf_op jit(solution)/shard_map/reduce_sum | solution.py:70
  206.3 44.6 %all-gather.3.cloned.1.call-done = bf16[6144,1024]{1,0:T(8,128)(2,1)} async-done(((bf16[192,1024]{1,0:T(8,128)(2,1)}), bf16[6144,1024]{1,0:T(8,128)(2,1)}) %all-gather.3.cloned.1.call-update) | async-done | bytes 12582928 | tf_op jit(solution)/shard_map/all_gather | solution.py:55
  250.8 16.7 %copy.13 = bf16[6144,1024]{0,1:T(8,128)(2,1)} copy(bf16[6144,1024]{1,0:T(8,128)(2,1)} %all-gather.3.cloned.1.call-done) | data formatting | bytes 25165824 | tf_op jit(solution)/shard_map/all_gather | solution.py:55
  267.6 29.8 %fusion.12 = bf16[192,16,64]{0,2,1:T(8,128)(2,1)S(1)} fusion(bf16[6144,16,64]{0,2,1:T(8,128)(2,1)} %bitcast.51, f32[16,192,6144]{2,1,0:T(8,128)} %get-tuple-element.39, f32[16,192]{1,0:T(8,128)S(1)} %broadcast_maximum_fusion, f32[192,16]{0,1:T(8,128)S(1)} %bitcast.54), kind=kOutput, calls=%fused_computation.41 | convolution fusion | flops 2472935424 | bytes 88498176 | tf_op jit(solution)/shard_map/hqk,khd->qhd/dot_general | solution.py:64
  297.4 0.7 fusion.108
  298.1 0.2 multiply_reduce_fusion.1
  298.3 0.2 multiply_multiply_fusion
  298.5 2.7 collective-permute-start
  301.2 1.9 collective-permute-start.1
  303.1 1.1 fusion.107
  304.3 2.5 collective-permute-done.1
  306.8 4.4 %multiply_add_fusion = f32[192,1024]{1,0:T(8,128)} fusion(f32[192,1024]{1,0:T(8,128)S(1)} %get-tuple-element.41, f32[15,1024]{1,0:T(8,128)S(1)} %collective-permute-done.1, f32[192,1024]{1,0:T(8,128)S(1)} %multiply_multiply_fusion, f32[15,1024]{1,0:T(8,128)S(1)} %collective-permute-done, f32[1024]{0:T(1024)S(1)} %bitcast.84, f32[1024]{0:T(1024)S(1)} %bitcast.85, ...), kind=kLoop, calls=%fused_computation.157 | loop fusion | flops 19070976 | bytes 2613248 | tf_op jit(solution)/shard_map/add | solution.py:85
  (19 shorter events, 0.1 us)
Async XLA Ops:
  6.5 290.8 %copy-start = (bf16[1024,1024]{1,0:T(8,128)(2,1)S(1)}, bf16[1024,1024]{1,0:T(8,128)(2,1)}, u32[]{:S(2)}) copy-start(bf16[1024,1024]{1,0:T(8,128)(2,1)} %param.14) | copy-start | bytes 6291460
  6.5 12.1 %copy-start.2 = (f32[31,1024]{1,0:T(8,128)S(1)}, f32[31,1024]{1,0:T(8,128)}, u32[]{:S(2)}) copy-start(f32[31,1024]{1,0:T(8,128)} %param.16) | copy-start | bytes 380932
  6.5 127.5 %all-gather.5.cloned.1.call-start = ((), (), s32[]{:S(2)}) async-start(), calls=%async_computation.1 | async-start | bytes 12976128 | tf_op jit(solution)/shard_map/all_gather | solution.py:51
  12.6 238.2 %all-gather.3.cloned.1.call-start = ((), (), s32[]{:S(2)}) async-start(), calls=%async_computation | async-start | bytes 12976128 | tf_op jit(solution)/shard_map/all_gather | solution.py:55
  267.5 29.8 %copy-start.1 = (f32[192,1024]{1,0:T(8,128)S(1)}, f32[192,1024]{1,0:T(8,128)}, u32[]{:S(2)}) copy-start(f32[192,1024]{1,0:T(8,128)} %param.9) | copy-start | bytes 2359300
  267.6 30.8 %copy-start.3 = (f32[1024]{0:T(1024)S(1)}, f32[1024]{0:T(1024)}, u32[]{:S(2)}) copy-start(f32[1024]{0:T(1024)} %param.15) | copy-start | bytes 12292
  267.6 39.2 %copy-start.4 = (f32[1024]{0:T(1024)S(1)}, f32[1024]{0:T(1024)}, u32[]{:S(2)}) copy-start(f32[1024]{0:T(1024)} %param.17) | copy-start | bytes 12292
  298.5 5.7 %collective-permute-start = (f32[15,1024]{1,0:T(8,128)S(1)}, f32[15,1024]{1,0:T(8,128)S(1)}, u32[]{:S(2)}, u32[]{:S(2)}) collective-permute-start(f32[15,1024]{1,0:T(8,128)S(1)} %get-tuple-element.5), channel_id=1, source_target_pairs={{0,1},{1,2},{2,3},{3,4},{4,5},{5,6},{6,7},{7,8},{8,9},{9,10},{10,1... | collective-permute-start | bytes 184328 | tf_op jit(solution)/shard_map/ppermute | solution.py:15
  301.2 5.6 %collective-permute-start.1 = (f32[15,1024]{1,0:T(8,128)S(1)}, f32[15,1024]{1,0:T(8,128)S(1)}, u32[]{:S(2)}, u32[]{:S(2)}) collective-permute-start(f32[15,1024]{1,0:T(8,128)S(1)} %get-tuple-element.6), channel_id=1, source_target_pairs={{1,0},{2,1},{3,2},{4,3},{5,4},{6,5},{7,6},{8,7},{9,8},{10,9},{11,1... | collective-permute-start | bytes 184328 | tf_op jit(solution)/shard_map/ppermute | solution.py:18
Sparse Core Ops, SparseCore 0:
  12.7 121.2 all-gather.4
  136.8 113.9 all-gather.2
where the time goes:
time: 319 us; the launch traced here: 318 us
  waiting for transfers between devices  162 us (51%)
  matrix products  69.8 us (22%)
  local copies, waits for them, and re-layouts  34.9 us (11%)
  other arithmetic  32.7 us (10%)
  between operations  13.5 us (4%)
  starting transfers between devices  4.63 us (1%)
    all_gather x1, waiting for transfers between devices, per_device(): key_block = lax.all_gather(key_rows, 'ctx', axis=0, tiled=True)  115 us
    all_gather x1, waiting for transfers between devices, per_device(): lax.all_gather(value_rows, 'ctx', axis=0, tiled=True)  44.6 us
    dot_general x1, matrix products, per_device(): jnp.einsum('qhd,khd->hqk', query_heads, key_heads, preferred_element_type...  30.4 us
    dot_general x1, matrix products, per_device(): jnp.einsum('hqk,khd->qhd', weights.astype(jnp.bfloat16), value_heads, pre...  29.8 us
    reduce_sum x1, other arithmetic, per_device(): totals = jnp.sum(weights, axis=2)  25.1 us
    all_gather x1, local copies, waits for them, and re-layouts, per_device(): key_block = lax.all_gather(key_rows, 'ctx', axis=0, tiled=True)  16.7 us
    all_gather x1, local copies, waits for them, and re-layouts, per_device(): lax.all_gather(value_rows, 'ctx', axis=0, tiled=True)  16.7 us
    dot_general x3, matrix products, project(): jnp.dot(source, weight, preferred_element_type=jnp.float32)  8.98 us
  transfers between devices with their start and end apart: 4, of which 3 were waited for; matrix products, arithmetic and copies ran while one was open for 25% of the time, Pallas kernels for 0%

commit v1 on v0

--- a/solution.py
+++ b/solution.py
@@ -1,3 +1,4 @@
+import functools
 import jax
 import jax.numpy as jnp
 from jax import lax
@@ -5,6 +6,22 @@
 
 HEADS = 16
 KERNEL = 31
+
+
+def point_floor(here_x, bus_axis):
+    everything = jnp.concatenate(
+        lax.all_to_all(
+            jnp.stack([here_x for _ in range(lax.axis_size(bus_axis))], axis=0),
+            axis_name=bus_axis,
+            split_axis=0,
+            concat_axis=0,
+        ),
+        0,
+    )
+    return everything
+
+
+carry_the_pieces_all = functools.partial(point_floor, bus_axis="ctx")
 
 
 def with_halo(block, sides, width):
@@ -52,9 +69,7 @@
     highest = jnp.full((HEADS, row_count), -1e30, jnp.float32)
     block_rows = key_block.shape[0]
     key_heads = key_block.reshape(block_rows, HEADS, head_size)
-    value_heads = lax.all_gather(value_rows, "ctx", axis=0, tiled=True).reshape(
-        block_rows, HEADS, head_size
-    )
+    value_heads = carry_the_pieces_all(value_rows).reshape(block_rows, HEADS, head_size)
     scores = (
         jnp.einsum("qhd,khd->hqk", query_heads, key_heads, preferred_element_type=jnp.float32)
         * score_scale

time: 319 us -> 530 us (1.66); the launches traced: 318 us -> 523 us
  waiting for transfers between devices: 162 us -> 311 us
  local copies, waits for them, and re-layouts: 34.9 us -> 76.6 us
  starting transfers between devices: 4.63 us -> 20.5 us
    all_to_all x0 -> x1, waiting for transfers between devices: none -> 311 us  [point_floor(): lax.all_to_all(jnp.stack([here_x for _ in range(lax.axis_size(bus_axis))]...]
    all_gather x1, waiting for transfers between devices: 115 us -> 0.01 us  [per_device(): key_block = lax.all_gather(key_rows, 'ctx', axis=0, tiled=True)]
    all_gather x1 -> x0, waiting for transfers between devices: 44.6 us -> none  [per_device(): lax.all_gather(value_rows, 'ctx', axis=0, tiled=True)]
    another operation x0 -> x2, local copies, waits for them, and re-layouts: none -> 32.6 us  [the longest x1 26.4 us: per_device(): carry_the_pieces_all(value_rows).reshape(block_rows, HEADS, head_size)]
    all_to_all x0 -> x1, local copies, waits for them, and re-layouts: none -> 24.3 us  [point_floor(): lax.all_to_all(jnp.stack([here_x for _ in range(lax.axis_size(bus_axis))]...]
    all_gather x1 -> x0, local copies, waits for them, and re-layouts: 16.7 us -> none  [per_device(): lax.all_gather(value_rows, 'ctx', axis=0, tiled=True)]
    all_to_all x0 -> x1, starting transfers between devices: none -> 12.7 us  [point_floor(): lax.all_to_all(jnp.stack([here_x for _ in range(lax.axis_size(bus_axis))]...]
  transfers between devices with their start and end apart: 4 -> 4, of which waited for: 3 -> 2; matrix products, arithmetic and copies ran while one was open for 25% -> 11% of each run, Pallas kernels for 0% -> 0%
where the time goes in v1:
time: 530 us; the launch traced here: 523 us
  waiting for transfers between devices  311 us (59%)
  local copies, waits for them, and re-layouts  76.6 us (14%)
  matrix products  68.9 us (13%)
  other arithmetic  32.1 us (6%)
  starting transfers between devices  20.5 us (4%)
  between operations  13.8 us (3%)
    all_to_all x1, waiting for transfers between devices, point_floor(): lax.all_to_all(jnp.stack([here_x for _ in range(lax.axis_size(bus_axis))]...  311 us
    dot_general x1, matrix products, per_device(): jnp.einsum('qhd,khd->hqk', query_heads, key_heads, preferred_element_type...  30.1 us
    dot_general x1, matrix products, per_device(): jnp.einsum('hqk,khd->qhd', weights.astype(jnp.bfloat16), value_heads, pre...  29.6 us
    another operation x1, local copies, waits for them, and re-layouts, per_device(): carry_the_pieces_all(value_rows).reshape(block_rows, HEADS, head_size)  26.4 us
    all_to_all x1, local copies, waits for them, and re-layouts, point_floor(): lax.all_to_all(jnp.stack([here_x for _ in range(lax.axis_size(bus_axis))]...  24.3 us
    reduce_sum x1, other arithmetic, per_device(): totals = jnp.sum(weights, axis=2)  23.7 us
    all_gather x1, local copies, waits for them, and re-layouts, per_device(): key_block = lax.all_gather(key_rows, 'ctx', axis=0, tiled=True)  16.6 us
    all_to_all x1, starting transfers between devices, point_floor(): lax.all_to_all(jnp.stack([here_x for _ in range(lax.axis_size(bus_axis))]...  12.7 us
  transfers between devices with their start and end apart: 4, of which 2 were waited for; matrix products, arithmetic and copies ran while one was open for 11% of the time, Pallas kernels for 0%

profile of v1, /device:TPU:1, one launch (start us, length us, event | category | flops | bytes accessed | tf_op | source)
XLA Modules:
  0.0 523.1 jit_solution(11825695588372493403)
XLA Ops:
  6.5 1.4 reduce_sum.45
  8.0 1.4 multiply_reduce_fusion.2
  9.3 2.5 convolution_convert_fusion.2
  11.8 6.1 %stack.2 = bf16[32,192,1024]{2,1,0:T(8,128)(2,1)} broadcast(bf16[192,1024]{1,0:T(8,128)(2,1)S(1)} %convolution_convert_fusion.2), dimensions={1,2} | broadcast | bytes 12976128 | tf_op jit(solution)/shard_map/stack | solution.py:14
  18.0 12.7 %all-to-all-start = ((bf16[32,192,1024]{2,1,0:T(8,128)(2,1)}), bf16[32,192,1024]{2,1,0:T(8,128)(2,1)}, u32[]{:S(2)}, u32[]{:S(2)}) async-start(bf16[32,192,1024]{2,1,0:T(8,128)(2,1)} %stack.2), calls=%async_computation | async-start | bytes 25165824 | tf_op jit(solution)/shard_map/all_to_all | solution.py:13
  30.8 3.0 convolution_convert_fusion
  33.8 3.0 convolution_convert_fusion.1
  36.8 1.2 copy.17
  38.0 0.7 fusion.106
  38.7 311.1 %all-to-all-done = bf16[32,192,1024]{2,1,0:T(8,128)(2,1)} async-done(((bf16[32,192,1024]{2,1,0:T(8,128)(2,1)}), bf16[32,192,1024]{2,1,0:T(8,128)(2,1)}, u32[]{:S(2)}, u32[]{:S(2)}) %all-to-all-start) | async-done | bytes 12582944 | tf_op jit(solution)/shard_map/all_to_all | solution.py:13
  349.8 24.3 %copy.16 = bf16[32,192,1024]{1,0,2:T(8,128)(2,1)} copy(bf16[32,192,1024]{2,1,0:T(8,128)(2,1)} %all-to-all-done) | data formatting | bytes 25165824 | tf_op jit(solution)/shard_map/all_to_all | solution.py:13
  374.1 26.4 %reshape_reshape.3 = bf16[6144,16,64]{0,2,1:T(8,128)(2,1)} reshape(bf16[32,192,1024]{1,0,2:T(8,128)(2,1)} %copy.16) | data formatting | bytes 25165824 | tf_op jit(solution)/shard_map/reshape;reshape | solution.py:72
  400.5 16.6 %copy.18 = bf16[6144,1024]{0,1:T(8,128)(2,1)} copy(bf16[6144,1024]{1,0:T(8,128)(2,1)} %all-gather.2.cloned.1.call-done) | data formatting | bytes 25165824 | tf_op jit(solution)/shard_map/all_gather | solution.py:68
  417.2 30.1 %multiply_reduce_fusion = (f32[16,192]{1,0:T(8,128)S(1)}, f32[16,192,6144]{2,1,0:T(8,128)}) fusion(bf16[192,16,64]{0,2,1:T(8,128)(2,1)S(1)} %bitcast.53, bf16[6144,16,64]{0,2,1:T(8,128)(2,1)} %bitcast.51), kind=kOutput, calls=%fused_computation.1 | convolution fusion | flops 2453664768 | bytes 88485888 | tf_op jit(solution)/shard_map/qhd,khd->hqk/dot_general | solution.py:74
  447.3 23.7 %fusion = f32[16,192]{1,0:T(8,128)S(1)} fusion(f32[16,192,6144]{2,1,0:T(8,128)} %get-tuple-element.39, f32[16,192]{1,0:T(8,128)S(1)} %broadcast_maximum_fusion), kind=kLoop, calls=%fused_computation.2 | loop fusion | flops 56620032 | bytes 75522048 | tf_op jit(solution)/shard_map/reduce_sum | solution.py:85
  471.2 29.6 %fusion.12 = bf16[192,16,64]{0,2,1:T(8,128)(2,1)S(1)} fusion(bf16[6144,16,64]{0,2,1:T(8,128)(2,1)} %reshape_reshape.3, f32[16,192,6144]{2,1,0:T(8,128)} %get-tuple-element.39, f32[16,192]{1,0:T(8,128)S(1)} %broadcast_maximum_fusion, f32[192,16]{0,1:T(8,128)S(1)} %bitcast.54), kind=kOutput, calls=%fused_computation.41 | convolution fusion | flops 2472935424 | bytes 88498176 | tf_op jit(solution)/shard_map/hqk,khd->qhd/dot_general | solution.py:79
  500.8 0.7 fusion.108
  501.5 0.2 multiply_reduce_fusion.1
  501.8 0.2 multiply_multiply_fusion
  502.0 5.7 %collective-permute-start.1 = (f32[15,1024]{1,0:T(8,128)S(1)}, f32[15,1024]{1,0:T(8,128)S(1)}, u32[]{:S(2)}, u32[]{:S(2)}) collective-permute-start(f32[15,1024]{1,0:T(8,128)S(1)} %get-tuple-element.6), channel_id=1, source_target_pairs={{1,0},{2,1},{3,2},{4,3},{5,4},{6,5},{7,6},{8,7},{9,8},{10,9},{11,1... | collective-permute-start | bytes 184328 | tf_op jit(solution)/shard_map/ppermute | solution.py:35
  507.7 1.9 collective-permute-start
  509.6 1.1 fusion.107
  510.8 0.2 collective-permute-done
  511.1 5.2 multiply_add_fusion
  (50 shorter events, 0.2 us)
Async XLA Ops:
  6.5 494.2 %copy-start = (bf16[1024,1024]{1,0:T(8,128)(2,1)S(1)}, bf16[1024,1024]{1,0:T(8,128)(2,1)}, u32[]{:S(2)}) copy-start(bf16[1024,1024]{1,0:T(8,128)(2,1)} %param.14) | copy-start | bytes 6291460
  18.0 12.8 %copy-start.1 = (f32[192,1024]{1,0:T(8,128)S(1)}, f32[192,1024]{1,0:T(8,128)}, u32[]{:S(2)}) copy-start(f32[192,1024]{1,0:T(8,128)} %param.9) | copy-start | bytes 2359300
  18.0 12.8 %copy-start.3 = (f32[1024]{0:T(1024)S(1)}, f32[1024]{0:T(1024)}, u32[]{:S(2)}) copy-start(f32[1024]{0:T(1024)} %param.10) | copy-start | bytes 12292
  18.0 20.0 %copy-start.2 = (f32[31,1024]{1,0:T(8,128)S(1)}, f32[31,1024]{1,0:T(8,128)}, u32[]{:S(2)}) copy-start(f32[31,1024]{1,0:T(8,128)} %param.16) | copy-start | bytes 380932
  18.0 331.8 %all-to-all-start = ((bf16[32,192,1024]{2,1,0:T(8,128)(2,1)}), bf16[32,192,1024]{2,1,0:T(8,128)(2,1)}, u32[]{:S(2)}, u32[]{:S(2)}) async-start(bf16[32,192,1024]{2,1,0:T(8,128)(2,1)} %stack.2), calls=%async_computation | async-start | bytes 25165824 | tf_op jit(solution)/shard_map/all_to_all | solution.py:13
  30.7 369.8 %all-gather.2.cloned.1.call-start = ((), (), s32[]{:S(2)}) async-start(), calls=%async_computation.1 | async-start | bytes 12976128 | tf_op jit(solution)/shard_map/all_gather | solution.py:68
  471.0 30.7 %copy-start.19 = (f32[1024]{0:T(1024)S(1)}, f32[1024]{0:T(1024)}, u32[]{:S(2)}) copy-start(f32[1024]{0:T(1024)} %param.15) | copy-start | bytes 12292
  471.1 39.9 %copy-start.4 = (f32[1,1024]{1,0:T(1,128)S(1)}, f32[1,1024]{1,0:T(1,128)}, u32[]{:S(2)}) copy-start(f32[1,1024]{1,0:T(1,128)} %get-tuple-element.11) | copy-start | bytes 12292
  471.1 39.9 %copy-start.5 = (f32[1,1024]{1,0:T(1,128)S(1)}, f32[1,1024]{1,0:T(1,128)}, u32[]{:S(2)}) copy-start(f32[1,1024]{1,0:T(1,128)} %get-tuple-element.12) | copy-start | bytes 12292
  471.1 39.9 %copy-start.6 = (f32[1,1024]{1,0:T(1,128)S(1)}, f32[1,1024]{1,0:T(1,128)}, u32[]{:S(2)}) copy-start(f32[1,1024]{1,0:T(1,128)} %get-tuple-element.13) | copy-start | bytes 12292
  471.1 39.9 %copy-start.7 = (f32[1,1024]{1,0:T(1,128)S(1)}, f32[1,1024]{1,0:T(1,128)}, u32[]{:S(2)}) copy-start(f32[1,1024]{1,0:T(1,128)} %get-tuple-element.14) | copy-start | bytes 12292
  471.1 39.9 %copy-start.8 = (f32[1,1024]{1,0:T(1,128)S(1)}, f32[1,1024]{1,0:T(1,128)}, u32[]{:S(2)}) copy-start(f32[1,1024]{1,0:T(1,128)} %get-tuple-element.15) | copy-start | bytes 12292
  471.1 39.9 %copy-start.9 = (f32[1,1024]{1,0:T(1,128)S(1)}, f32[1,1024]{1,0:T(1,128)}, u32[]{:S(2)}) copy-start(f32[1,1024]{1,0:T(1,128)} %get-tuple-element.16) | copy-start | bytes 12292
  471.1 39.9 %copy-start.10 = (f32[1,1024]{1,0:T(1,128)S(1)}, f32[1,1024]{1,0:T(1,128)}, u32[]{:S(2)}) copy-start(f32[1,1024]{1,0:T(1,128)} %get-tuple-element.17) | copy-start | bytes 12292
  471.1 39.9 %copy-start.11 = (f32[1,1024]{1,0:T(1,128)S(1)}, f32[1,1024]{1,0:T(1,128)}, u32[]{:S(2)}) copy-start(f32[1,1024]{1,0:T(1,128)} %get-tuple-element.18) | copy-start | bytes 12292
  471.1 39.9 %copy-start.12 = (f32[1,1024]{1,0:T(1,128)S(1)}, f32[1,1024]{1,0:T(1,128)}, u32[]{:S(2)}) copy-start(f32[1,1024]{1,0:T(1,128)} %get-tuple-element.19) | copy-start | bytes 12292
  471.1 39.9 %copy-start.13 = (f32[1,1024]{1,0:T(1,128)S(1)}, f32[1,1024]{1,0:T(1,128)}, u32[]{:S(2)}) copy-start(f32[1,1024]{1,0:T(1,128)} %get-tuple-element.20) | copy-start | bytes 12292
  471.2 39.9 %copy-start.14 = (f32[1,1024]{1,0:T(1,128)S(1)}, f32[1,1024]{1,0:T(1,128)}, u32[]{:S(2)}) copy-start(f32[1,1024]{1,0:T(1,128)} %get-tuple-element.21) | copy-start | bytes 12292
  471.2 39.9 %copy-start.15 = (f32[1,1024]{1,0:T(1,128)S(1)}, f32[1,1024]{1,0:T(1,128)}, u32[]{:S(2)}) copy-start(f32[1,1024]{1,0:T(1,128)} %get-tuple-element.22) | copy-start | bytes 12292
  471.2 39.9 %copy-start.16 = (f32[1,1024]{1,0:T(1,128)S(1)}, f32[1,1024]{1,0:T(1,128)}, u32[]{:S(2)}) copy-start(f32[1,1024]{1,0:T(1,128)} %get-tuple-element.23) | copy-start | bytes 12292
  471.2 39.9 %copy-start.17 = (f32[1,1024]{1,0:T(1,128)S(1)}, f32[1,1024]{1,0:T(1,128)}, u32[]{:S(2)}) copy-start(f32[1,1024]{1,0:T(1,128)} %get-tuple-element.24) | copy-start | bytes 12292
  471.2 39.9 %copy-start.18 = (f32[1,1024]{1,0:T(1,128)S(1)}, f32[1,1024]{1,0:T(1,128)}, u32[]{:S(2)}) copy-start(f32[1,1024]{1,0:T(1,128)} %get-tuple-element.25) | copy-start | bytes 12292
  502.0 8.8 %collective-permute-start.1 = (f32[15,1024]{1,0:T(8,128)S(1)}, f32[15,1024]{1,0:T(8,128)S(1)}, u32[]{:S(2)}, u32[]{:S(2)}) collective-permute-start(f32[15,1024]{1,0:T(8,128)S(1)} %get-tuple-element.6), channel_id=1, source_target_pairs={{1,0},{2,1},{3,2},{4,3},{5,4},{6,5},{7,6},{8,7},{9,8},{10,9},{11,1... | collective-permute-start | bytes 184328 | tf_op jit(solution)/shard_map/ppermute | solution.py:35
  507.7 3.2 collective-permute-start
Sparse Core Ops, SparseCore 0:
  34.3 251.2 all-gather.1
